TPU v7x, 32 devices: a whole 2x2x4 slice. The times are simulated.
32 devices in a mesh: groups: 2 (over y), row: 4 (over x, core), col: 4 (over z).
Axes of the slice: x: 2, y: 2, z: 4, core: 2. Of those that a mesh axis runs over, the one named last changes fastest.
Arguments:
- right_sides: float32 [32, 16384], P(None, ('groups', 'row')), parts along dimension 1
- nugget: float32 [16384], P(('groups', 'row')), parts along dimension 0, may hold values from 1 to 4
- cov_blocks: bfloat16 [8, 4, 32, 256, 256], P(('groups', 'row'), 'col'), parts along dimension 0
- block_rows: int32 [8, 4, 32], P(('groups', 'row'), 'col'), parts along dimension 0, may hold values from 0 to 7, as said below
- block_cols: int32 [8, 4, 32], P(('groups', 'row'), 'col'), parts along dimension 0, may hold values from 0 to 7, as said below
- block_count: int32 [8, 4], P(('groups', 'row'), 'col'), parts along dimension 0, may hold values from 4 to 32, as said below
Outputs:
- solution: float32 [32, 16384], P(None, ('groups', 'row')), parts along dimension 1
- residual: float32 [32, 16384], P(None, ('groups', 'row')), parts along dimension 1
There are 2 independent parts, one for each index of `groups`. A program takes and returns all parts, laid end to end along the dimension named above; each array names one. Nothing has to cross between parts.
Inputs may be any that keep to these rules, and one draw needn't show every extreme that they name: On each device the pairs (block_rows, block_cols) of all 32 slots are distinct; no stored block position of a problem is the mirror image of another (no pair is stored both as (g, h) and as (h, g)); on devices whose row and col index are equal, block_rows <= block_cols. `block_cols`: see block_rows. `block_count`: slots at or beyond the count are empty; some device of every problem has exactly 32 live slots.
All inputs are finite; a program needn't handle non-finite values.
Results may differ from a plain program's by a relative error of at most 0.0003.
Values sent between devices are 32-bit elements; how exact they have to be, the bound alone decides.
A program may use at most 64 MiB of HBM per device.

v0:
```python
import jax
import jax.numpy as jnp
from jax import lax
from jax.sharding import PartitionSpec as P

ITERS = 2


def from_root(value, axis, source):
    kept = jnp.where(lax.axis_index(axis) == source, value, 0).astype(value.dtype)
    return lax.psum(kept, axis)


def on_device(right_sides, nugget, cov_blocks, block_rows, block_cols, block_count):
    blocks = cov_blocks[0, 0].astype(jnp.float32)
    slot_rows = block_rows[0, 0]
    slot_cols = block_cols[0, 0]
    live_count = block_count[0, 0]
    slot_total = blocks.shape[0]
    tile_size = blocks.shape[1]
    series, row_width = right_sides.shape
    tile_count = row_width // tile_size
    live_mask = (jnp.arange(slot_total, dtype=jnp.int32) < live_count).astype(jnp.float32)
    block_ids = jnp.arange(tile_count, dtype=jnp.int32)[:, None]
    row_selector = (slot_rows[None, :] == block_ids).astype(jnp.float32) * live_mask[None, :]
    col_selector = (slot_cols[None, :] == block_ids).astype(jnp.float32) * live_mask[None, :]

    def spread(selector, values):
        placed = jnp.einsum("bm,rmj->rbj", selector, values, precision=lax.Precision.HIGHEST)
        return placed.reshape(series, row_width)

    solution = jnp.zeros_like(right_sides)
    residual = right_sides
    direction = right_sides
    norm_now = lax.psum(jnp.sum(residual * residual, axis=1), "row")
    for turn_index in range(ITERS):
        far_rows = from_root(direction, "row", lax.axis_index("col"))
        near_tiles = direction.reshape(series, tile_count, tile_size)
        far_tiles = far_rows.reshape(series, tile_count, tile_size)
        local_direct = jnp.einsum(
            "rmk,mjk->rmj",
            jnp.take(far_tiles, slot_cols, axis=1),
            blocks,
            precision=lax.Precision.HIGHEST,
        )
        local_mirror = jnp.einsum(
            "rmj,mjk->rmk",
            jnp.take(near_tiles, slot_rows, axis=1),
            blocks,
            precision=lax.Precision.HIGHEST,
        )
        apply_direct = spread(row_selector, local_direct)
        apply_mirror = spread(col_selector, local_mirror)
        total = lax.psum(apply_direct, "col")
        summed = lax.psum(apply_mirror, "row")
        total = total + from_root(summed, "col", lax.axis_index("row"))
        applied = nugget[None, :] * direction + total
        curvature, crossed, squared = lax.psum(
            (
                jnp.sum(direction * applied, axis=1),
                jnp.sum(residual * applied, axis=1),
                jnp.sum(applied * applied, axis=1),
            ),
            "row",
        )
        step_size = norm_now / curvature
        solution = solution + step_size[:, None] * direction
        residual = residual - step_size[:, None] * applied
        norm_next = norm_now - 2.0 * step_size * crossed + step_size * step_size * squared
        direction = residual + (norm_next / norm_now)[:, None] * direction
        norm_now = norm_next
    return (solution, residual)


def solution(mesh):
    placed = (
        P(None, ("groups", "row")),
        P(("groups", "row")),
        P(("groups", "row"), "col", None, None, None),
        P(("groups", "row"), "col", None),
        P(("groups", "row"), "col", None),
        P(("groups", "row"), "col"),
    )
    return jax.shard_map(
        on_device,
        mesh=mesh,
        in_specs=placed,
        out_specs=(P(None, ("groups", "row")), P(None, ("groups", "row"))),
        check_vma=False,
    )
```

profile of v0, /device:TPU:0, one launch (start us, length us, event | category | flops | bytes accessed | tf_op | source)
XLA Modules:
  0.0 210.6 jit_solution(2557300919919235164)
XLA Ops:
  9.2 1.0 copy.38
  10.2 1.0 broadcast_select_fusion.1
  12.5 4.4 %fusion.11 = f32[32,32,256]{2,0,1:T(8,128)S(1)} fusion(bf16[1,1,32,256,256]{4,3,2,1,0:T(8,128)(2,1)} %param.10, f32[32,32,256]{2,1,0:T(8,128)S(1)} %gather_fusion.1, pred[32]{0:T(512)(128)(4,1)S(1)} %compare_and_fusion), kind=kOutput, calls=%fused_computation.13 | convolution fusion | flops 805568512 | bytes 6291488 | tf_op jit(solution)/shard_map/rmj,mjk->rmk/dot_general | solution.py:46
  16.9 1.2 fusion.28
  18.2 0.8 copy.21
  19.1 35.7 %all-reduce.14.cloned.1.call-done = (f32[32,8,256]{2,0,1:T(8,128)}, f32[32,2048]{1,0:T(8,128)}) async-done(((f32[32,8,256]{2,0,1:T(8,128)}, f32[32,2048]{1,0:T(8,128)}), (f32[32,8,256]{2,0,1:T(8,128)}, f32[32,2048]{1,0:T(8,128)})) %all-reduce.14.cloned.1.call-update) | async-done | bytes 524304 | tf_op jit(solution)/shard_map/psum | solution.py:11
  54.8 1.6 gather_fusion
  56.4 6.0 %fusion.8 = f32[32,32,256]{2,0,1:T(8,128)S(1)} fusion(bf16[1,1,32,256,256]{4,3,2,1,0:T(8,128)(2,1)} %param.10, f32[32,32,256]{2,1,0:T(8,128)S(1)} %gather_fusion, pred[32]{0:T(512)(128)(4,1)S(1)} %compare_and_fusion.1), kind=kOutput, calls=%fused_computation.12 | convolution fusion | flops 805568512 | bytes 6291488 | tf_op jit(solution)/shard_map/rmk,mjk->rmj/dot_general | solution.py:40
  62.4 1.2 fusion.30
  64.6 35.8 %all-reduce.8.cloned.1.call-done = f32[32,2048]{1,0:T(8,128)} async-done(((f32[32,2048]{1,0:T(8,128)}), f32[32,2048]{1,0:T(8,128)}) %all-reduce.8.cloned.1.call-update) | async-done | bytes 262160 | tf_op jit(solution)/shard_map/psum | solution.py:54
  100.4 1.2 multiply_reduce_fusion.2
  101.6 5.7 %all-reduce = (f32[32]{0:T(128)S(1)}, f32[32]{0:T(128)S(1)}, f32[32]{0:T(128)S(1)}) all-reduce(f32[32]{0:T(128)S(1)} %get-tuple-element.4, f32[32]{0:T(128)S(1)} %get-tuple-element.5, f32[32]{0:T(128)S(1)} %get-tuple-element.3), channel_id=1, replica_groups=mesh['groups'=2,'row'=4,'col'=4] {'row'}, use_global_device_ids=true, to_apply=%region_9.11 | all-reduce | flops 96 | bytes 768 | tf_op jit(solution)/shard_map/psum | solution.py:58
  107.3 1.1 broadcast_select_fusion
  109.7 4.4 %fusion.17 = f32[32,32,256]{2,0,1:T(8,128)S(1)} fusion(bf16[1,1,32,256,256]{4,3,2,1,0:T(8,128)(2,1)} %param.10, f32[32,32,256]{2,1,0:T(8,128)S(1)} %gather_fusion.3, pred[32]{0:T(512)(128)(4,1)S(1)} %compare_and_fusion), kind=kOutput, calls=%fused_computation.15 | convolution fusion | flops 805568512 | bytes 6291488 | tf_op jit(solution)/shard_map/rmj,mjk->rmk/dot_general | solution.py:46
  114.1 1.2 fusion.24
  115.3 0.8 copy.23
  116.4 33.5 %all-reduce.12.cloned.1.call-done = (f32[32,8,256]{2,0,1:T(8,128)}, f32[32,2048]{1,0:T(8,128)}) async-done(((f32[32,8,256]{2,0,1:T(8,128)}, f32[32,2048]{1,0:T(8,128)}), (f32[32,8,256]{2,0,1:T(8,128)}, f32[32,2048]{1,0:T(8,128)})) %all-reduce.12.cloned.1.call-update) | async-done | bytes 524304 | tf_op jit(solution)/shard_map/psum | solution.py:11
  149.9 1.6 gather_fusion.2
  151.5 6.0 %fusion.14 = f32[32,32,256]{2,0,1:T(8,128)S(1)} fusion(bf16[1,1,32,256,256]{4,3,2,1,0:T(8,128)(2,1)} %param.10, f32[32,32,256]{2,1,0:T(8,128)S(1)} %gather_fusion.2, pred[32]{0:T(512)(128)(4,1)S(1)} %compare_and_fusion.1), kind=kOutput, calls=%fused_computation.14 | convolution fusion | flops 805568512 | bytes 6291488 | tf_op jit(solution)/shard_map/rmk,mjk->rmj/dot_general | solution.py:40
  157.5 1.2 fusion.26
  159.6 35.9 %all-reduce.10.cloned.1.call-done = f32[32,2048]{1,0:T(8,128)} async-done(((f32[32,2048]{1,0:T(8,128)}), f32[32,2048]{1,0:T(8,128)}) %all-reduce.10.cloned.1.call-update) | async-done | bytes 262160 | tf_op jit(solution)/shard_map/psum | solution.py:54
  195.4 1.1 multiply_reduce_fusion
  196.5 5.7 %psum.98 = f32[32]{0:T(128)S(1)} all-reduce(f32[32]{0:T(128)S(1)} %multiply_reduce_fusion), channel_id=1, replica_groups=mesh['groups'=2,'row'=4,'col'=4] {'row'}, use_global_device_ids=true, to_apply=%region_15.17 | all-reduce | flops 32 | bytes 256 | tf_op jit(solution)/shard_map/psum | solution.py:58
  202.2 1.9 multiply_subtract_fusion
  (40 shorter events, 6.2 us)
Async XLA Ops:
  7.2 47.6 %all-reduce.14.cloned.1.call-start = ((), (), s32[]{:S(2)}) async-start(), calls=%async_computation.3 | async-start | bytes 1048576 | tf_op jit(solution)/shard_map/psum | solution.py:11
  11.9 5.0 %copy-start.5 = (s32[1,1,32]{2,1,0:T(1,128)S(1)}, s32[1,1,32]{2,1,0:T(1,128)}, u32[]{:S(2)}) copy-start(s32[1,1,32]{2,1,0:T(1,128)} %param.12) | copy-start | bytes 388
  19.0 81.4 %all-reduce.8.cloned.1.call-start = ((), (), s32[]{:S(2)}) async-start(), calls=%async_computation | async-start | bytes 524288 | tf_op jit(solution)/shard_map/psum | solution.py:54
  54.8 7.6 %copy-start.6 = (s32[1,1,32]{2,1,0:T(1,128)S(1)}, s32[1,1,32]{2,1,0:T(1,128)}, u32[]{:S(2)}) copy-start(s32[1,1,32]{2,1,0:T(1,128)} %param.11) | copy-start | bytes 388
  56.4 7.4 %copy-start.2 = (f32[32,2048]{1,0:T(8,128)S(1)}, f32[32,2048]{1,0:T(8,128)}, u32[]{:S(2)}) copy-start(f32[32,2048]{1,0:T(8,128)} %get-tuple-element.12) | copy-start | bytes 786436
  56.4 44.0 %copy-start = (f32[32,2048]{1,0:T(8,128)S(1)}, f32[32,2048]{1,0:T(8,128)}, u32[]{:S(2)}) copy-start(f32[32,2048]{1,0:T(8,128)} %param.8) | copy-start | bytes 786436
  56.4 44.0 %copy-start.4 = (f32[2048]{0:T(1024)S(1)}, f32[2048]{0:T(1024)}, u32[]{:S(2)}) copy-start(f32[2048]{0:T(1024)} %param.9) | copy-start | bytes 24580
  64.5 85.4 %all-reduce.12.cloned.1.call-start = ((), (), s32[]{:S(2)}) async-start(), calls=%async_computation.2 | async-start | bytes 1048576 | tf_op jit(solution)/shard_map/psum | solution.py:11
  116.1 79.3 %all-reduce.10.cloned.1.call-start = ((), (), s32[]{:S(2)}) async-start(), calls=%async_computation.1 | async-start | bytes 524288 | tf_op jit(solution)/shard_map/psum | solution.py:54
  151.5 7.4 %copy-start.3 = (f32[32,2048]{1,0:T(8,128)S(1)}, f32[32,2048]{1,0:T(8,128)}, u32[]{:S(2)}) copy-start(f32[32,2048]{1,0:T(8,128)} %get-tuple-element.10) | copy-start | bytes 786436
  151.5 50.7 %copy-start.1 = (f32[32,2048]{1,0:T(8,128)S(1)}, f32[32,2048]{1,0:T(8,128)}, u32[]{:S(2)}) copy-start(f32[32,2048]{1,0:T(8,128)} %all-reduce.8.cloned.1.call-done) | copy-start | bytes 786436
Sparse Core Ops, SparseCore 0:
  19.1 35.6 all-reduce.13
  64.6 35.7 all-reduce.7
  116.3 33.5 all-reduce.11
  159.7 35.6 all-reduce.9
where the time goes:
time: 211 us
  waiting for transfers between devices  141 us (67%)
  matrix products  25.7 us (12%)
  between operations  14.7 us (7%)
  blocking collectives  11.3 us (5%)
  other arithmetic  9.03 us (4%)
  local copies, waits for them, and re-layouts  8.58 us (4%)
    psum x2, waiting for transfers between devices, on_device(): total = lax.psum(apply_direct, 'col')  71.7 us
    psum x2, waiting for transfers between devices, from_root(): return lax.psum(kept, axis)  69.2 us
    dot_general x2, matrix products, on_device(): jnp.einsum('rmk,mjk->rmj', jnp.take(far_tiles, slot_cols, axis=1), blocks...  12 us
    psum x2, blocking collectives, on_device(): lax.psum((jnp.sum(direction * applied, axis=1), jnp.sum(residual * applie...  11.3 us
    dot_general x2, matrix products, on_device(): jnp.einsum('rmj,mjk->rmk', jnp.take(near_tiles, slot_rows, axis=1), block...  8.74 us
    dot_general x4, matrix products, spread(): jnp.einsum('bm,rmj->rbj', selector, values, precision=lax.Precision.HIGHEST)  4.95 us
  transfers between devices with their start and end apart: 4, of which 4 were waited for; matrix products, arithmetic and copies ran while one was open for 0% of the time, Pallas kernels for 0%

commit v1 on v0

--- a/solution.py
+++ b/solution.py
@@ -4,6 +4,17 @@
 from jax.sharding import PartitionSpec as P
 
 ITERS = 2
+
+
+def widths_lift(packet):
+    k_all = lax.axis_size("col")
+    after = lambda plain: [(kk, kk ^ plain) for kk in range(k_all)]
+    newest = packet
+    for ix in range(k_all.bit_length() - 1):
+        arr_out = after(1 << ix)
+        kept_arr = lax.ppermute(newest, "col", arr_out)
+        newest = newest + kept_arr
+    return newest
 
 
 def from_root(value, axis, source):
@@ -51,7 +62,7 @@
         )
         apply_direct = spread(row_selector, local_direct)
         apply_mirror = spread(col_selector, local_mirror)
-        total = lax.psum(apply_direct, "col")
+        total = widths_lift(apply_direct)
         summed = lax.psum(apply_mirror, "row")
         total = total + from_root(summed, "col", lax.axis_index("row"))
         applied = nugget[None, :] * direction + total

time: 211 us -> 226 us (1.071)
  starting transfers between devices: 0.35 us -> 8.89 us
  waiting for transfers between devices: 141 us -> 148 us
    ppermute x0 -> x4, waiting for transfers between devices: none -> 9.22 us  [widths_lift(): kept_arr = lax.ppermute(newest, 'col', arr_out)]
    ppermute x0 -> x4, starting transfers between devices: none -> 8.55 us  [widths_lift(): kept_arr = lax.ppermute(newest, 'col', arr_out)]
    psum x2, waiting for transfers between devices: 71.7 us -> 69.3 us  [on_device(): summed = lax.psum(apply_mirror, 'row')]
  transfers between devices with their start and end apart: 4 -> 8, of which waited for: 4 -> 6; matrix products, arithmetic and copies ran while one was open for 0% -> 1% of each run, Pallas kernels for 0% -> 0%
where the time goes in v1:
time: 226 us; the launch traced here: 225 us
  waiting for transfers between devices  148 us (65%)
  matrix products  25.6 us (11%)
  between operations  14.7 us (7%)
  blocking collectives  11.3 us (5%)
  starting transfers between devices  8.89 us (4%)
  local copies, waits for them, and re-layouts  8.58 us (4%)
  other arithmetic  8.14 us (4%)
    psum x2, waiting for transfers between devices, from_root(): return lax.psum(kept, axis)  69.3 us
    psum x2, waiting for transfers between devices, on_device(): summed = lax.psum(apply_mirror, 'row')  69.3 us
    dot_general x2, matrix products, on_device(): jnp.einsum('rmk,mjk->rmj', jnp.take(far_tiles, slot_cols, axis=1), blocks...  12 us
    psum x2, blocking collectives, on_device(): lax.psum((jnp.sum(direction * applied, axis=1), jnp.sum(residual * applie...  11.3 us
    ppermute x4, waiting for transfers between devices, widths_lift(): kept_arr = lax.ppermute(newest, 'col', arr_out)  9.22 us
    dot_general x2, matrix products, on_device(): jnp.einsum('rmj,mjk->rmk', jnp.take(near_tiles, slot_rows, axis=1), block...  8.74 us
    ppermute x4, starting transfers between devices, widths_lift(): kept_arr = lax.ppermute(newest, 'col', arr_out)  8.55 us
    dot_general x4, matrix products, spread(): jnp.einsum('bm,rmj->rbj', selector, values, precision=lax.Precision.HIGHEST)  4.95 us
  transfers between devices with their start and end apart: 8, of which 6 were waited for; matrix products, arithmetic and copies ran while one was open for 1% of the time, Pallas kernels for 0%

profile of v1, /device:TPU:0, one launch (start us, length us, event | category | flops | bytes accessed | tf_op | source)
XLA Modules:
  0.0 225.1 jit_solution(2256271047653826565)
XLA Ops:
  12.5 4.4 %fusion.11 = f32[32,32,256]{2,0,1:T(8,128)S(1)} fusion(bf16[1,1,32,256,256]{4,3,2,1,0:T(8,128)(2,1)} %param.10, f32[32,32,256]{2,1,0:T(8,128)S(1)} %gather_fusion.1, pred[32]{0:T(512)(128)(4,1)S(1)} %compare_and_fusion), kind=kOutput, calls=%fused_computation.13 | convolution fusion | flops 805568512 | bytes 6291488 | tf_op jit(solution)/shard_map/rmj,mjk->rmk/dot_general | solution.py:57
  16.9 1.2 fusion.28
  19.1 35.7 %all-reduce.14.cloned.1.call-done = (f32[32,2048]{1,0:T(8,128)}, f32[32,8,256]{2,0,1:T(8,128)}) async-done(((f32[32,2048]{1,0:T(8,128)}, f32[32,8,256]{2,0,1:T(8,128)}), (f32[32,2048]{1,0:T(8,128)}, f32[32,8,256]{2,0,1:T(8,128)})) %all-reduce.14.cloned.1.call-update) | async-done | bytes 524304 | tf_op jit(solution)/shard_map/psum | solution.py:66
  54.8 1.6 gather_fusion
  56.4 6.0 %fusion.8 = f32[32,32,256]{2,0,1:T(8,128)S(1)} fusion(bf16[1,1,32,256,256]{4,3,2,1,0:T(8,128)(2,1)} %param.10, f32[32,32,256]{2,1,0:T(8,128)S(1)} %gather_fusion, pred[32]{0:T(512)(128)(4,1)S(1)} %compare_and_fusion.1), kind=kOutput, calls=%fused_computation.12 | convolution fusion | flops 805568512 | bytes 6291488 | tf_op jit(solution)/shard_map/rmk,mjk->rmj/dot_general | solution.py:51
  62.4 1.2 fusion.30
  63.7 1.6 collective-permute-start
  66.1 4.6 %collective-permute-done = f32[32,2048]{1,0:T(8,128)S(1)} collective-permute-done((f32[32,2048]{1,0:T(8,128)S(1)}, f32[32,2048]{1,0:T(8,128)S(1)}, u32[]{:S(2)}, u32[]{:S(2)}) %collective-permute-start) | collective-permute-done | bytes 262176 | tf_op jit(solution)/shard_map/ppermute | solution.py:15
  70.7 2.7 %collective-permute-start.1 = (f32[32,2048]{1,0:T(8,128)S(1)}, f32[32,2048]{1,0:T(8,128)S(1)}, u32[]{:S(2)}, u32[]{:S(2)}) collective-permute-start(f32[32,2048]{1,0:T(8,128)S(1)} %add.60), channel_id=1, source_target_pairs={{0,2},{1,3},{2,0},{3,1},{4,6},{5,7},{6,4},{7,5},{8,10},{9,11},{10,... | collective-permute-start | bytes 786440 | tf_op jit(solution)/shard_map/ppermute | solution.py:15
  73.4 34.6 %all-reduce.8.cloned.1.call-done = f32[32,2048]{1,0:T(8,128)} async-done(((f32[32,2048]{1,0:T(8,128)}), f32[32,2048]{1,0:T(8,128)}) %all-reduce.8.cloned.1.call-update) | async-done | bytes 262160 | tf_op jit(solution)/shard_map/psum | solution.py:22
  108.1 1.2 multiply_reduce_fusion.2
  109.3 5.7 %all-reduce = (f32[32]{0:T(128)S(1)}, f32[32]{0:T(128)S(1)}, f32[32]{0:T(128)S(1)}) all-reduce(f32[32]{0:T(128)S(1)} %get-tuple-element.4, f32[32]{0:T(128)S(1)} %get-tuple-element.5, f32[32]{0:T(128)S(1)} %get-tuple-element.3), channel_id=1, replica_groups=mesh['groups'=2,'row'=4,'col'=4] {'row'}, use_global_device_ids=true, to_apply=%region_8.10 | all-reduce | flops 96 | bytes 768 | tf_op jit(solution)/shard_map/psum | solution.py:69
  116.4 4.4 %fusion.17 = f32[32,32,256]{2,0,1:T(8,128)S(1)} fusion(bf16[1,1,32,256,256]{4,3,2,1,0:T(8,128)(2,1)} %param.10, f32[32,32,256]{2,1,0:T(8,128)S(1)} %gather_fusion.3, pred[32]{0:T(512)(128)(4,1)S(1)} %compare_and_fusion), kind=kOutput, calls=%fused_computation.15 | convolution fusion | flops 805568512 | bytes 6291488 | tf_op jit(solution)/shard_map/rmj,mjk->rmk/dot_general | solution.py:57
  120.8 1.2 fusion.24
  123.1 33.5 %all-reduce.12.cloned.1.call-done = (f32[32,2048]{1,0:T(8,128)}, f32[32,8,256]{2,0,1:T(8,128)}) async-done(((f32[32,2048]{1,0:T(8,128)}, f32[32,8,256]{2,0,1:T(8,128)}), (f32[32,2048]{1,0:T(8,128)}, f32[32,8,256]{2,0,1:T(8,128)})) %all-reduce.12.cloned.1.call-update) | async-done | bytes 524304 | tf_op jit(solution)/shard_map/psum | solution.py:66
  156.6 1.6 gather_fusion.2
  158.2 6.0 %fusion.14 = f32[32,32,256]{2,0,1:T(8,128)S(1)} fusion(bf16[1,1,32,256,256]{4,3,2,1,0:T(8,128)(2,1)} %param.10, f32[32,32,256]{2,1,0:T(8,128)S(1)} %gather_fusion.2, pred[32]{0:T(512)(128)(4,1)S(1)} %compare_and_fusion.1), kind=kOutput, calls=%fused_computation.14 | convolution fusion | flops 805568512 | bytes 6291488 | tf_op jit(solution)/shard_map/rmk,mjk->rmj/dot_general | solution.py:51
  164.2 1.2 fusion.26
  165.5 1.6 collective-permute-start.2
  167.8 4.6 %collective-permute-done.2 = f32[32,2048]{1,0:T(8,128)S(1)} collective-permute-done((f32[32,2048]{1,0:T(8,128)S(1)}, f32[32,2048]{1,0:T(8,128)S(1)}, u32[]{:S(2)}, u32[]{:S(2)}) %collective-permute-start.2) | collective-permute-done | bytes 262176 | tf_op jit(solution)/shard_map/ppermute | solution.py:15
  172.5 2.7 %collective-permute-start.3 = (f32[32,2048]{1,0:T(8,128)S(1)}, f32[32,2048]{1,0:T(8,128)S(1)}, u32[]{:S(2)}, u32[]{:S(2)}) collective-permute-start(f32[32,2048]{1,0:T(8,128)S(1)} %add.66), channel_id=1, source_target_pairs={{0,2},{1,3},{2,0},{3,1},{4,6},{5,7},{6,4},{7,5},{8,10},{9,11},{10,... | collective-permute-start | bytes 786440 | tf_op jit(solution)/shard_map/ppermute | solution.py:15
  175.2 34.6 %all-reduce.10.cloned.1.call-done = f32[32,2048]{1,0:T(8,128)} async-done(((f32[32,2048]{1,0:T(8,128)}), f32[32,2048]{1,0:T(8,128)}) %all-reduce.10.cloned.1.call-update) | async-done | bytes 262160 | tf_op jit(solution)/shard_map/psum | solution.py:22
  211.0 5.7 %psum.82 = f32[32]{0:T(128)S(1)} all-reduce(f32[32]{0:T(128)S(1)} %multiply_reduce_fusion), channel_id=1, replica_groups=mesh['groups'=2,'row'=4,'col'=4] {'row'}, use_global_device_ids=true, to_apply=%region_13.15 | all-reduce | flops 32 | bytes 256 | tf_op jit(solution)/shard_map/psum | solution.py:69
  216.7 1.9 multiply_subtract_fusion
  (48 shorter events, 10.9 us)
Async XLA Ops:
  7.2 47.6 %all-reduce.14.cloned.1.call-start = ((), (), s32[]{:S(2)}) async-start(), calls=%async_computation.3 | async-start | bytes 1048576 | tf_op jit(solution)/shard_map/psum | solution.py:66
  11.9 5.0 %copy-start.4 = (s32[1,1,32]{2,1,0:T(1,128)S(1)}, s32[1,1,32]{2,1,0:T(1,128)}, u32[]{:S(2)}) copy-start(s32[1,1,32]{2,1,0:T(1,128)} %param.12) | copy-start | bytes 388
  19.0 89.1 %all-reduce.8.cloned.1.call-start = ((), (), s32[]{:S(2)}) async-start(), calls=%async_computation | async-start | bytes 524288 | tf_op jit(solution)/shard_map/psum | solution.py:22
  54.8 7.6 %copy-start.5 = (s32[1,1,32]{2,1,0:T(1,128)S(1)}, s32[1,1,32]{2,1,0:T(1,128)}, u32[]{:S(2)}) copy-start(s32[1,1,32]{2,1,0:T(1,128)} %param.11) | copy-start | bytes 388
  56.4 8.9 %copy-start.1 = (f32[32,2048]{1,0:T(8,128)S(1)}, f32[32,2048]{1,0:T(8,128)}, u32[]{:S(2)}) copy-start(f32[32,2048]{1,0:T(8,128)} %get-tuple-element.11) | copy-start | bytes 786436
  56.4 51.7 %copy-start = (f32[32,2048]{1,0:T(8,128)S(1)}, f32[32,2048]{1,0:T(8,128)}, u32[]{:S(2)}) copy-start(f32[32,2048]{1,0:T(8,128)} %param.8) | copy-start | bytes 786436
  56.4 51.7 %copy-start.3 = (f32[2048]{0:T(1024)S(1)}, f32[2048]{0:T(1024)}, u32[]{:S(2)}) copy-start(f32[2048]{0:T(1024)} %param.9) | copy-start | bytes 24580
  63.7 6.9 %collective-permute-start = (f32[32,2048]{1,0:T(8,128)S(1)}, f32[32,2048]{1,0:T(8,128)S(1)}, u32[]{:S(2)}, u32[]{:S(2)}) collective-permute-start(f32[32,2048]{1,0:T(8,128)S(1)} %bitcast.89), channel_id=1, source_target_pairs={{0,1},{1,0},{2,3},{3,2},{4,5},{5,4},{6,7},{7,6},{8,9},{9,8},{10,11... | collective-permute-start | bytes 786440 | tf_op jit(solution)/shard_map/ppermute | solution.py:15
  66.0 90.6 %all-reduce.12.cloned.1.call-start = ((), (), s32[]{:S(2)}) async-start(), calls=%async_computation.2 | async-start | bytes 1048576 | tf_op jit(solution)/shard_map/psum | solution.py:66
  70.7 37.4 %collective-permute-start.1 = (f32[32,2048]{1,0:T(8,128)S(1)}, f32[32,2048]{1,0:T(8,128)S(1)}, u32[]{:S(2)}, u32[]{:S(2)}) collective-permute-start(f32[32,2048]{1,0:T(8,128)S(1)} %add.60), channel_id=1, source_target_pairs={{0,2},{1,3},{2,0},{3,1},{4,6},{5,7},{6,4},{7,5},{8,10},{9,11},{10,... | collective-permute-start | bytes 786440 | tf_op jit(solution)/shard_map/ppermute | solution.py:15
  122.9 87.0 %all-reduce.10.cloned.1.call-start = ((), (), s32[]{:S(2)}) async-start(), calls=%async_computation.1 | async-start | bytes 524288 | tf_op jit(solution)/shard_map/psum | solution.py:22
  158.2 8.9 %copy-start.2 = (f32[32,2048]{1,0:T(8,128)S(1)}, f32[32,2048]{1,0:T(8,128)}, u32[]{:S(2)}) copy-start(f32[32,2048]{1,0:T(8,128)} %get-tuple-element.9) | copy-start | bytes 786436
  165.5 6.9 %collective-permute-start.2 = (f32[32,2048]{1,0:T(8,128)S(1)}, f32[32,2048]{1,0:T(8,128)S(1)}, u32[]{:S(2)}, u32[]{:S(2)}) collective-permute-start(f32[32,2048]{1,0:T(8,128)S(1)} %bitcast.91), channel_id=1, source_target_pairs={{0,1},{1,0},{2,3},{3,2},{4,5},{5,4},{6,7},{7,6},{8,9},{9,8},{10,11... | collective-permute-start | bytes 786440 | tf_op jit(solution)/shard_map/ppermute | solution.py:15
  172.5 37.4 %collective-permute-start.3 = (f32[32,2048]{1,0:T(8,128)S(1)}, f32[32,2048]{1,0:T(8,128)S(1)}, u32[]{:S(2)}, u32[]{:S(2)}) collective-permute-start(f32[32,2048]{1,0:T(8,128)S(1)} %add.66), channel_id=1, source_target_pairs={{0,2},{1,3},{2,0},{3,1},{4,6},{5,7},{6,4},{7,5},{8,10},{9,11},{10,... | collective-permute-start | bytes 786440 | tf_op jit(solution)/shard_map/ppermute | solution.py:15
Sparse Core Ops, SparseCore 0:
  19.1 35.6 all-reduce.13
  66.2 41.8 all-reduce.7
  123.0 33.5 all-reduce.11
  168.0 41.8 all-reduce.9
